TPU v7x, 32 devices: a whole 2x2x4 slice. The times are simulated.
32 devices in a mesh: seq: 16 (over z, y, x), grp: 2 (over core).
Axes of the slice: x: 2, y: 2, z: 4, core: 2. Of those that a mesh axis runs over, the one named last changes fastest.
Arguments:
- key_rows: bfloat16 [32768, 4096], P('seq', 'grp')
- probe_ints: int32 [4096, 512], P('grp'), may hold values from -2 to 2
- rank_keep: int32 [1], replicated, may hold values from 128 to 511
Outputs:
- latents: float32 [32768, 512], P('seq', 'grp')
- latent_basis: float32 [512, 4096], P('seq', 'grp')
All inputs are finite; a program needn't handle non-finite values.
Results may differ from a plain program's by a relative error of at most 0.00098.
Values may be sent and summed in bfloat16 or wider, within the bound.
A program may use at most 128 MiB of HBM per device.

v0:
```python
import math
import jax
import jax.numpy as jnp
from jax import lax
from jax.sharding import PartitionSpec as P


def on_device(key_rows, probe_ints, rank_keep):
    seq_count = lax.axis_size("seq")
    tokens = key_rows.shape[0] * seq_count
    root_tokens = math.sqrt(tokens)
    probes = (probe_ints.astype(jnp.float32) * 0.015625).astype(jnp.bfloat16)
    whole_keys = lax.all_gather(key_rows, "grp", axis=1, tiled=True)
    whole_probes = lax.all_gather(probes, "grp", axis=0, tiled=True)
    sketch = jnp.dot(whole_keys, whole_probes, preferred_element_type=jnp.float32)
    contract = (((0,), (0,)), ((), ()))
    local_gram = lax.dot_general(sketch, sketch, contract, precision=lax.Precision.HIGHEST)
    gram_matrix = lax.psum(local_gram, "seq")
    lower_factor = jnp.linalg.cholesky(gram_matrix)
    identity = jnp.eye(gram_matrix.shape[0], dtype=jnp.float32)
    inverse = lax.linalg.triangular_solve(lower_factor, identity, left_side=True, lower=True)
    orthonormal = jnp.dot(sketch, inverse.T, precision=lax.Precision.HIGHEST) * root_tokens
    probe_count = orthonormal.shape[1]
    part_width = probe_count // lax.axis_size("grp")
    first_column = lax.axis_index("grp") * part_width
    columns = first_column + jnp.arange(part_width)
    own_columns = lax.dynamic_slice_in_dim(orthonormal, first_column, part_width, 1)
    latents = jnp.where(columns[None, :] < rank_keep[0], own_columns, jnp.float32(0.0))
    rounded = orthonormal.astype(jnp.bfloat16)
    rows_out = probe_count // seq_count
    summed = lax.psum_scatter(
        lax.dot_general(rounded, key_rows, contract, preferred_element_type=jnp.float32),
        "seq",
        scatter_dimension=0,
        tiled=True,
    )
    row_index = lax.axis_index("seq") * rows_out + jnp.arange(rows_out)
    latent_basis = jnp.where(
        row_index[:, None] < rank_keep[0], summed / root_tokens, jnp.float32(0.0)
    )
    return (latents, latent_basis)


def solution(mesh):
    in_specs = (P("seq", "grp"), P("grp", None), P())
    out_specs = (P("seq", "grp"), P("seq", "grp"))
    return jax.shard_map(
        on_device, mesh=mesh, in_specs=in_specs, out_specs=out_specs, check_vma=False
    )
```

profile of v0, /device:TPU:0, one launch (start us, length us, event | category | flops | bytes accessed | tf_op | source)
XLA Modules:
  0.0 463.2 jit_solution(5321967595677841850)
XLA Ops:
  7.2 0.0 all-gather.3.cloned.1.call-start
  7.2 4.1 multiply_convert_fusion
  11.3 0.0 all-gather.3.cloned.1.call-update
  11.3 0.0 all-gather.5.cloned.1.call-start
  11.4 0.7 all-gather.5.cloned.1.call-update
  12.1 0.0 all-reduce.3.cloned.1.call-start
  12.1 15.7 %all-gather.3.cloned.1.call-done = bf16[4096,512]{1,0:T(8,128)(2,1)} async-done(((bf16[2048,512]{1,0:T(8,128)(2,1)}), bf16[4096,512]{1,0:T(8,128)(2,1)}) %all-gather.3.cloned.1.call-update) | async-done | bytes 4194320 | tf_op jit(solution)/shard_map/all_gather | solution.py:14
  27.8 32.8 %all-gather.5.cloned.1.call-done = bf16[2048,4096]{1,0:T(8,128)(2,1)} async-done(((bf16[2048,2048]{1,0:T(8,128)(2,1)}), bf16[2048,4096]{1,0:T(8,128)(2,1)}) %all-gather.5.cloned.1.call-update) | async-done | bytes 16777232 | tf_op jit(solution)/shard_map/all_gather | solution.py:13
  60.7 13.0 %fusion.42 = f32[512,2048]{1,0:T(8,128)S(1)} fusion(bf16[4096,512]{1,0:T(8,128)(2,1)} %all-gather.3.cloned.1.call-done, bf16[2048,4096]{1,0:T(8,128)(2,1)} %all-gather.5.cloned.1.call-done), kind=kOutput, calls=%fused_computation.84 | convolution fusion | flops 8589934592 | bytes 25165824 | tf_op jit(solution)/shard_map/dot_general | solution.py:15
  73.7 1.9 copy-done
  75.7 7.7 %fusion.43 = f32[512,512]{0,1:T(8,128)} fusion(f32[512,2048]{1,0:T(8,128)S(1)} %fusion.42), kind=kOutput, calls=%fused_computation.85 | convolution fusion | flops 6442450944 | bytes 5242880 | tf_op jit(solution)/shard_map/dot_general | solution.py:17
  83.4 0.0 all-reduce.3.cloned.1.call-update
  83.4 0.2 reduce-scatter.2.cloned.1.call-start
  83.6 0.8 iota_compare_fusion
  84.4 0.1 fusion.18
  84.5 111.9 %all-reduce.3.cloned.1.call-done = f32[512,512]{0,1:T(8,128)} async-done(((f32[512,512]{0,1:T(8,128)}), f32[512,512]{0,1:T(8,128)}) %all-reduce.3.cloned.1.call-update) | async-done | bytes 1048592 | tf_op jit(solution)/shard_map/psum | solution.py:18
  196.4 1.6 copy.6
  198.0 1.4 fusion.9
  199.5 11.7 %cholesky.104 = f32[128,128]{1,0:T(8,128)S(1)} custom-call(f32[128,128]{1,0:T(8,128)S(1)} %cholesky.266), custom_call_target="Cholesky" | custom-call | tf_op jit(solution)/shard_map/jit(cholesky)/cholesky | solution.py:19
  211.2 9.8 %custom-call.30 = f32[1,128,128]{1,2,0:T(8,128)S(1)} custom-call(f32[1,128,128]{2,1,0:T(8,128)S(1)} %get-tuple-element.29), custom_call_target="InvertDiagBlocksLowerTriangular" | custom-call | tf_op jit(solution)/shard_map/jit(cholesky)/cholesky | solution.py:19
  221.0 0.1 cholesky.224
  221.2 0.3 constant_dynamic-update-slice_fusion.2
  221.5 0.3 convolution_subtract_fusion.3
  221.8 11.7 %cholesky.217 = f32[128,128]{1,0:T(8,128)S(1)} custom-call(f32[128,128]{1,0:T(8,128)S(1)} %cholesky.270), custom_call_target="Cholesky" | custom-call | tf_op jit(solution)/shard_map/jit(cholesky)/cholesky | solution.py:19
  233.6 10.2 %custom-call.31 = f32[1,128,128]{1,2,0:T(8,128)S(1)} custom-call(f32[1,128,128]{2,1,0:T(8,128)S(1)} %get-tuple-element.26), custom_call_target="InvertDiagBlocksLowerTriangular" | custom-call | tf_op jit(solution)/shard_map/jit(cholesky)/cholesky | solution.py:19
  243.8 0.3 convolution_dynamic-update-slice_fusion
  244.0 0.4 convolution_subtract_fusion.4
  244.4 11.7 %cholesky.238 = f32[128,128]{1,0:T(8,128)S(1)} custom-call(f32[128,128]{1,0:T(8,128)S(1)} %cholesky.275), custom_call_target="Cholesky" | custom-call | tf_op jit(solution)/shard_map/jit(cholesky)/cholesky | solution.py:19
  256.2 0.7 compare_reduce_fusion.1
  256.8 9.8 %custom-call.32 = f32[1,128,128]{1,2,0:T(8,128)S(1)} custom-call(f32[1,128,128]{2,1,0:T(8,128)S(1)} %get-tuple-element.23), custom_call_target="InvertDiagBlocksLowerTriangular" | custom-call | tf_op jit(solution)/shard_map/jit(cholesky)/cholesky | solution.py:19
  266.7 0.2 convolution_dynamic-update-slice_fusion.1
  266.9 0.4 convolution_subtract_fusion.5
  267.3 11.7 %cholesky.255 = f32[128,128]{1,0:T(8,128)S(1)} custom-call(f32[128,128]{1,0:T(8,128)S(1)} %convolution_subtract_fusion.5), custom_call_target="Cholesky" | custom-call | tf_op jit(solution)/shard_map/jit(cholesky)/cholesky | solution.py:19
  279.0 0.7 compare_reduce_fusion
  279.7 0.9 compare_reduce_fusion.2
  283.1 0.1 select_select_fusion
  283.3 10.3 %while.1 = (s32[]{:T(128)}, f32[512,512]{1,0:T(8,128)S(1)}, s32[4,2]{0,1:T(2,128)S(1)}, f32[4,128,128]{2,1,0:T(8,128)}, s32[]{:T(128)}) while((s32[]{:T(128)}, f32[512,512]{1,0:T(8,128)S(1)}, s32[4,2]{0,1:T(2,128)S(1)}, f32[4,128,128]{2,1,0:T(8,128)}, s32[]{:T(128)}) %tuple.31), condition=%wide.while_cond, body=%wide.while_body.sunk | while | flops 2 | bytes 132705 | solution.py:21
  283.3 0.1 constant_dynamic-slice_fusion.2
  283.3 0.5 fusion.56
  283.9 2.0 bitcast_dynamic-update-slice_fusion.2
  285.9 0.1 constant_dynamic-slice_fusion.2
  285.9 0.5 fusion.56
  286.4 2.0 bitcast_dynamic-update-slice_fusion.2
  288.4 0.1 constant_dynamic-slice_fusion.2
  288.5 0.5 fusion.56
  289.0 2.0 bitcast_dynamic-update-slice_fusion.2
  291.0 0.1 constant_dynamic-slice_fusion.2
  291.1 0.5 fusion.56
  291.6 2.0 bitcast_dynamic-update-slice_fusion.2
  293.6 40.1 %custom-call.33 = f32[4,128,128]{1,2,0:T(8,128)S(1)} custom-call(f32[4,128,128]{2,1,0:T(8,128)} %get-tuple-element.9), custom_call_target="InvertDiagBlocksLowerTriangular" | custom-call | tf_op jit(solution)/shard_map/triangular_solve | solution.py:21
  333.7 1.2 fusion.20
  334.9 0.4 convolution_subtract_fusion.1
  335.3 0.4 fusion.32
  335.7 0.4 convolution_subtract_fusion
  336.2 0.4 fusion.30
  336.6 0.6 convolution_subtract_fusion.2
  337.3 0.4 fusion.29
  337.7 14.6 %convolution_multiply_fusion = f32[2048,512]{1,0:T(8,128)S(1)} fusion(f32[512,2048]{1,0:T(8,128)S(1)} %copy-done.1, f32[128,512]{1,0:T(8,128)S(1)} %fusion.29, f32[128,512]{1,0:T(8,128)S(1)} %fusion.30, f32[128,512]{1,0:T(8,128)S(1)} %fusion.32, f32[128,512]{1,0:T(8,128)S(1)} %fusion.20), kind=kOutput, calls=%fused_computation.3 | convolution fusion | flops 6444285952 | bytes 9437184 | tf_op jit(solution)/shard_map/dot_general | solution.py:22
  352.3 1.9 copy-done.2
  354.2 6.1 %fusion = f32[512,2048]{1,0:T(8,128)} fusion(bf16[2048,2048]{1,0:T(8,128)(2,1)S(1)} %bitcast.58, f32[2048,512]{1,0:T(8,128)S(1)} %convolution_multiply_fusion), kind=kOutput, calls=%fused_computation.4 | convolution fusion | flops 4296015872 | bytes 16777216 | tf_op jit(solution)/shard_map/dot_general | solution.py:32
  360.3 0.0 reduce-scatter.2.cloned.1.call-update
  361.0 3.1 dynamic-slice_select_fusion
  364.1 90.6 %reduce-scatter.2.cloned.1.call-done = f32[32,2048]{1,0:T(8,128)} async-done(((f32[512,2048]{1,0:T(8,128)}), f32[32,2048]{1,0:T(8,128)}) %reduce-scatter.2.cloned.1.call-update) | async-done | bytes 262160 | tf_op jit(solution)/shard_map/reduce_scatter | solution.py:31
  454.7 1.7 multiply_select_fusion
  (21 shorter events, 0.2 us)
Async XLA Ops:
  7.2 20.7 %all-gather.3.cloned.1.call-start = ((), (), s32[]{:S(2)}) async-start(), calls=%async_computation.1 | async-start | bytes 6291456 | tf_op jit(solution)/shard_map/all_gather | solution.py:14
  11.3 49.4 %all-gather.5.cloned.1.call-start = ((), (), s32[]{:S(2)}) async-start(), calls=%async_computation.2 | async-start | bytes 25165824 | tf_op jit(solution)/shard_map/all_gather | solution.py:13
  12.1 184.4 %all-reduce.3.cloned.1.call-start = ((), (), s32[]{:S(2)}) async-start(), calls=%async_computation.3 | async-start | bytes 2097152 | tf_op jit(solution)/shard_map/psum | solution.py:18
  73.7 1.9 copy-start
  83.4 371.3 %reduce-scatter.2.cloned.1.call-start = ((), (), s32[]{:S(2)}) async-start(), calls=%async_computation.4 | async-start | bytes 4456448 | tf_op jit(solution)/shard_map/reduce_scatter | solution.py:31
  333.7 4.0 copy-start.1
  336.6 17.6 %slice-start = ((s8[8388608]{0:T(1024)(128)(4,1)}), s8[4194304]{0:T(1024)(128)(4,1)S(1)}, s32[]{:S(2)}) async-start(s8[8388608]{0:T(1024)(128)(4,1)} %bitcast.57), calls=%async_computation.5 | async-start | bytes 8388608
  337.7 16.5 %slice-start.1 = ((s8[8388608]{0:T(1024)(128)(4,1)}), s8[4194304]{0:T(1024)(128)(4,1)S(1)}, s32[]{:S(2)}) async-start(s8[8388608]{0:T(1024)(128)(4,1)} %bitcast.57), calls=%async_computation.6 | async-start | bytes 8388608
  352.3 1.9 copy-start.2
Sparse Core Ops, SparseCore 0:
  11.4 16.3 all-gather.2
  29.4 31.2 all-gather.4
  83.5 112.8 all-reduce.2
  360.4 94.2 reduce-scatter.1
where the time goes:
time: 471 us; the launch traced here: 463 us
  waiting for transfers between devices  252 us (54%)
  other arithmetic  130 us (28%)
  matrix products  47.2 us (10%)
  between operations  17.5 us (4%)
  local copies, waits for them, and re-layouts  15.8 us (3%)
    psum x1, waiting for transfers between devices, on_device(): gram_matrix = lax.psum(local_gram, 'seq')  112 us
    reduce_scatter x1, waiting for transfers between devices, on_device(): lax.psum_scatter(lax.dot_general(rounded, key_rows, contract, preferred_e...  90.6 us
    another operation x14, other arithmetic, on_device(): lower_factor = jnp.linalg.cholesky(gram_matrix)  79 us
    another operation x3, other arithmetic, on_device(): lax.linalg.triangular_solve(lower_factor, identity, left_side=True, lower...  40.3 us
    all_gather x1, waiting for transfers between devices, on_device(): whole_keys = lax.all_gather(key_rows, 'grp', axis=1, tiled=True)  32.8 us
    all_gather x1, waiting for transfers between devices, on_device(): whole_probes = lax.all_gather(probes, 'grp', axis=0, tiled=True)  15.7 us
    dot_general x1, matrix products, on_device(): jnp.dot(sketch, inverse.T, precision=lax.Precision.HIGHEST) * root_tokens  14.6 us
    dot_general x1, matrix products, on_device(): jnp.dot(whole_keys, whole_probes, preferred_element_type=jnp.float32)  13 us
  transfers between devices with their start and end apart: 4, of which 4 were waited for; matrix products, arithmetic and copies ran while one was open for 1% of the time, Pallas kernels for 0%

commit v1 on v0

--- a/solution.py
+++ b/solution.py
@@ -15,7 +15,11 @@
     sketch = jnp.dot(whole_keys, whole_probes, preferred_element_type=jnp.float32)
     contract = (((0,), (0,)), ((), ()))
     local_gram = lax.dot_general(sketch, sketch, contract, precision=lax.Precision.HIGHEST)
-    gram_matrix = lax.psum(local_gram, "seq")
+    gram_matrix = local_gram
+    for hop in (1, 2, 4, 8):
+        gram_matrix = gram_matrix + lax.ppermute(
+            gram_matrix, "seq", [(dev, dev ^ hop) for dev in range(16)]
+        )
     lower_factor = jnp.linalg.cholesky(gram_matrix)
     identity = jnp.eye(gram_matrix.shape[0], dtype=jnp.float32)
     inverse = lax.linalg.triangular_solve(lower_factor, identity, left_side=True, lower=True)

time: 471 us -> 476 us (1.011)
  starting transfers between devices: 0.34 us -> 8.27 us
    psum x1 -> x0, waiting for transfers between devices: 112 us -> none  [on_device(): gram_matrix = lax.psum(local_gram, 'seq')]
    ppermute x0 -> x4, waiting for transfers between devices: none -> 112 us  [on_device(): lax.ppermute(gram_matrix, 'seq', [(dev, dev ^ hop) for dev in range(16)])]
    ppermute x0 -> x4, starting transfers between devices: none -> 8.15 us  [on_device(): lax.ppermute(gram_matrix, 'seq', [(dev, dev ^ hop) for dev in range(16)])]
  transfers between devices with their start and end apart: 4 -> 7, of which waited for: 4 -> 7; matrix products, arithmetic and copies ran while one was open for 1% -> 1% of each run, Pallas kernels for 0% -> 0%
where the time goes in v1:
time: 476 us; the launch traced here: 473 us
  waiting for transfers between devices  254 us (53%)
  other arithmetic  131 us (28%)
  matrix products  49.2 us (10%)
  between operations  17.4 us (4%)
  local copies, waits for them, and re-layouts  13.5 us (3%)
  starting transfers between devices  8.27 us (2%)
    ppermute x4, waiting for transfers between devices, on_device(): lax.ppermute(gram_matrix, 'seq', [(dev, dev ^ hop) for dev in range(16)])  112 us
    reduce_scatter x1, waiting for transfers between devices, on_device(): lax.psum_scatter(lax.dot_general(rounded, key_rows, contract, preferred_e...  92.7 us
    another operation x14, other arithmetic, on_device(): lower_factor = jnp.linalg.cholesky(gram_matrix)  79 us
    another operation x3, other arithmetic, on_device(): lax.linalg.triangular_solve(lower_factor, identity, left_side=True, lower...  40.4 us
    all_gather x1, waiting for transfers between devices, on_device(): whole_keys = lax.all_gather(key_rows, 'grp', axis=1, tiled=True)  32.8 us
    all_gather x1, waiting for transfers between devices, on_device(): whole_probes = lax.all_gather(probes, 'grp', axis=0, tiled=True)  15.7 us
    dot_general x1, matrix products, on_device(): jnp.dot(sketch, inverse.T, precision=lax.Precision.HIGHEST) * root_tokens  14.6 us
    dot_general x1, matrix products, on_device(): jnp.dot(whole_keys, whole_probes, preferred_element_type=jnp.float32)  13.2 us
  transfers between devices with their start and end apart: 7, of which 7 were waited for; matrix products, arithmetic and copies ran while one was open for 1% of the time, Pallas kernels for 0%

profile of v1, /device:TPU:0, one launch (start us, length us, event | category | flops | bytes accessed | tf_op | source)
XLA Modules:
  0.0 472.8 jit_solution(11982758630215182708)
XLA Ops:
  7.2 4.1 multiply_convert_fusion
  11.4 0.7 all-gather.5.cloned.1.call-update
  12.1 15.7 %all-gather.3.cloned.1.call-done = bf16[4096,512]{1,0:T(8,128)(2,1)} async-done(((bf16[2048,512]{1,0:T(8,128)(2,1)}), bf16[4096,512]{1,0:T(8,128)(2,1)}) %all-gather.3.cloned.1.call-update) | async-done | bytes 4194320 | tf_op jit(solution)/shard_map/all_gather | solution.py:14
  27.8 32.8 %all-gather.5.cloned.1.call-done = bf16[2048,4096]{1,0:T(8,128)(2,1)} async-done(((bf16[2048,2048]{1,0:T(8,128)(2,1)}), bf16[2048,4096]{1,0:T(8,128)(2,1)}) %all-gather.5.cloned.1.call-update) | async-done | bytes 16777232 | tf_op jit(solution)/shard_map/all_gather | solution.py:13
  60.7 13.2 %fusion.47 = f32[512,2048]{1,0:T(8,128)S(1)} fusion(bf16[4096,512]{1,0:T(8,128)(2,1)} %all-gather.3.cloned.1.call-done, bf16[2048,4096]{1,0:T(8,128)(2,1)} %all-gather.5.cloned.1.call-done), kind=kOutput, calls=%fused_computation.87 | convolution fusion | flops 8589934592 | bytes 25165824 | tf_op jit(solution)/shard_map/dot_general | solution.py:15
  73.9 6.7 %fusion.48 = f32[512,512]{0,1:T(8,128)S(1)} fusion(f32[512,2048]{1,0:T(8,128)S(1)} %fusion.47), kind=kOutput, calls=%fused_computation.88 | convolution fusion | flops 6442450944 | bytes 5242880 | tf_op jit(solution)/shard_map/dot_general | solution.py:17
  80.7 1.8 collective-permute-start
  82.5 23.6 %collective-permute-done = f32[512,512]{0,1:T(8,128)S(1)} collective-permute-done((f32[512,512]{0,1:T(8,128)S(1)}, f32[512,512]{0,1:T(8,128)S(1)}, u32[]{:S(2)}, u32[]{:S(2)}) %collective-permute-start) | collective-permute-done | bytes 1048608 | tf_op jit(solution)/shard_map/ppermute | solution.py:20
  106.1 0.2 add.79
  106.3 1.8 collective-permute-start.1
  108.1 22.8 %collective-permute-done.1 = f32[512,512]{0,1:T(8,128)S(1)} collective-permute-done((f32[512,512]{0,1:T(8,128)S(1)}, f32[512,512]{0,1:T(8,128)S(1)}, u32[]{:S(2)}, u32[]{:S(2)}) %collective-permute-start.1) | collective-permute-done | bytes 1048608 | tf_op jit(solution)/shard_map/ppermute | solution.py:20
  130.9 0.2 add.80
  131.1 1.8 collective-permute-start.2
  133.0 21.9 %collective-permute-done.2 = f32[512,512]{0,1:T(8,128)S(1)} collective-permute-done((f32[512,512]{0,1:T(8,128)S(1)}, f32[512,512]{0,1:T(8,128)S(1)}, u32[]{:S(2)}, u32[]{:S(2)}) %collective-permute-start.2) | collective-permute-done | bytes 1048608 | tf_op jit(solution)/shard_map/ppermute | solution.py:20
  154.8 0.2 add.81
  155.1 2.7 collective-permute-start.3
  157.8 0.1 iota_compare_fusion
  157.9 0.1 fusion.18
  158.0 43.3 %collective-permute-done.3 = f32[512,512]{0,1:T(8,128)} collective-permute-done((f32[512,512]{0,1:T(8,128)S(1)}, f32[512,512]{0,1:T(8,128)}, u32[]{:S(2)}, u32[]{:S(2)}) %collective-permute-start.3) | collective-permute-done | bytes 1048608 | tf_op jit(solution)/shard_map/ppermute | solution.py:20
  201.3 1.4 add.82
  202.8 0.3 copy.7
  203.1 0.2 fusion.9
  203.3 1.0 copy-done.3
  204.3 11.9 %cholesky.104 = f32[128,128]{1,0:T(8,128)S(1)} custom-call(f32[128,128]{1,0:T(8,128)S(1)} %cholesky.266), custom_call_target="Cholesky" | custom-call | tf_op jit(solution)/shard_map/jit(cholesky)/cholesky | solution.py:23
  216.3 9.8 %custom-call.30 = f32[1,128,128]{1,2,0:T(8,128)S(1)} custom-call(f32[1,128,128]{2,1,0:T(8,128)S(1)} %get-tuple-element.29), custom_call_target="InvertDiagBlocksLowerTriangular" | custom-call | tf_op jit(solution)/shard_map/jit(cholesky)/cholesky | solution.py:23
  226.1 0.1 cholesky.224
  226.2 1.2 constant_dynamic-update-slice_fusion.2
  227.5 1.3 slice_subtract_fusion
  228.7 11.7 %cholesky.217 = f32[128,128]{1,0:T(8,128)S(1)} custom-call(f32[128,128]{1,0:T(8,128)S(1)} %cholesky.270), custom_call_target="Cholesky" | custom-call | tf_op jit(solution)/shard_map/jit(cholesky)/cholesky | solution.py:23
  240.5 9.8 %custom-call.31 = f32[1,128,128]{1,2,0:T(8,128)S(1)} custom-call(f32[1,128,128]{2,1,0:T(8,128)S(1)} %get-tuple-element.26), custom_call_target="InvertDiagBlocksLowerTriangular" | custom-call | tf_op jit(solution)/shard_map/jit(cholesky)/cholesky | solution.py:23
  250.3 0.3 convolution_dynamic-update-slice_fusion
  250.6 1.3 slice_subtract_fusion.1
  251.9 12.1 %cholesky.238 = f32[128,128]{1,0:T(8,128)S(1)} custom-call(f32[128,128]{1,0:T(8,128)S(1)} %cholesky.275), custom_call_target="Cholesky" | custom-call | tf_op jit(solution)/shard_map/jit(cholesky)/cholesky | solution.py:23
  264.0 0.6 compare_reduce_fusion.1
  264.7 9.8 %custom-call.32 = f32[1,128,128]{1,2,0:T(8,128)S(1)} custom-call(f32[1,128,128]{2,1,0:T(8,128)S(1)} %get-tuple-element.23), custom_call_target="InvertDiagBlocksLowerTriangular" | custom-call | tf_op jit(solution)/shard_map/jit(cholesky)/cholesky | solution.py:23
  274.5 0.2 convolution_dynamic-update-slice_fusion.1
  274.7 1.2 slice_subtract_fusion.2
  275.9 11.7 %cholesky.255 = f32[128,128]{1,0:T(8,128)S(1)} custom-call(f32[128,128]{1,0:T(8,128)S(1)} %slice_subtract_fusion.2), custom_call_target="Cholesky" | custom-call | tf_op jit(solution)/shard_map/jit(cholesky)/cholesky | solution.py:23
  287.7 0.6 compare_reduce_fusion
  288.3 0.7 compare_reduce_fusion.2
  291.5 0.1 select_select_fusion
  291.6 10.1 %while.1 = (s32[]{:T(128)}, f32[512,512]{1,0:T(8,128)S(1)}, s32[4,2]{0,1:T(2,128)S(1)}, f32[4,128,128]{2,1,0:T(8,128)}, s32[]{:T(128)}) while((s32[]{:T(128)}, f32[512,512]{1,0:T(8,128)S(1)}, s32[4,2]{0,1:T(2,128)S(1)}, f32[4,128,128]{2,1,0:T(8,128)}, s32[]{:T(128)}) %tuple.31), condition=%wide.while_cond, body=%wide.while_body.sunk | while | flops 2 | bytes 132705 | solution.py:25
  291.7 0.5 fusion.61
  292.2 1.9 bitcast_dynamic-update-slice_fusion.2
  294.2 0.5 fusion.61
  294.7 1.9 bitcast_dynamic-update-slice_fusion.2
  296.8 0.5 fusion.61
  297.3 1.9 bitcast_dynamic-update-slice_fusion.2
  299.3 0.5 fusion.61
  299.8 1.9 bitcast_dynamic-update-slice_fusion.2
  301.7 40.3 %custom-call.33 = f32[4,128,128]{1,2,0:T(8,128)S(1)} custom-call(f32[4,128,128]{2,1,0:T(8,128)} %get-tuple-element.9), custom_call_target="InvertDiagBlocksLowerTriangular" | custom-call | tf_op jit(solution)/shard_map/triangular_solve | solution.py:25
  342.1 0.3 fusion.21
  342.4 0.4 convolution_subtract_fusion.1
  342.8 0.4 fusion.34
  343.2 0.4 convolution_subtract_fusion
  343.6 0.4 fusion.32
  344.1 0.6 convolution_subtract_fusion.2
  344.7 0.4 fusion.31
  345.1 14.6 %convolution_multiply_fusion = f32[2048,512]{1,0:T(8,128)S(1)} fusion(f32[512,2048]{1,0:T(8,128)S(1)} %copy-done.1, f32[128,512]{1,0:T(8,128)S(1)} %fusion.31, f32[128,512]{1,0:T(8,128)S(1)} %fusion.32, f32[128,512]{1,0:T(8,128)S(1)} %fusion.34, f32[128,512]{1,0:T(8,128)S(1)} %fusion.21), kind=kOutput, calls=%fused_computation.3 | convolution fusion | flops 6444285952 | bytes 9437184 | tf_op jit(solution)/shard_map/dot_general | solution.py:26
  359.7 1.9 copy-done.2
  361.7 6.2 %fusion = f32[512,2048]{1,0:T(8,128)} fusion(bf16[2048,2048]{1,0:T(8,128)(2,1)S(1)} %bitcast.58, f32[2048,512]{1,0:T(8,128)S(1)} %convolution_multiply_fusion), kind=kOutput, calls=%fused_computation.4 | convolution fusion | flops 4296015872 | bytes 16777216 | tf_op jit(solution)/shard_map/dot_general | solution.py:36
  368.6 3.1 dynamic-slice_select_fusion
  371.7 92.7 %reduce-scatter.2.cloned.1.call-done = f32[32,2048]{1,0:T(8,128)} async-done(((f32[512,2048]{1,0:T(8,128)}), f32[32,2048]{1,0:T(8,128)}) %reduce-scatter.2.cloned.1.call-update) | async-done | bytes 262160 | tf_op jit(solution)/shard_map/reduce_scatter | solution.py:35
  464.3 1.7 multiply_select_fusion
  (32 shorter events, 0.7 us)
Async XLA Ops:
  7.2 20.7 %all-gather.3.cloned.1.call-start = ((), (), s32[]{:S(2)}) async-start(), calls=%async_computation.1 | async-start | bytes 6291456 | tf_op jit(solution)/shard_map/all_gather | solution.py:14
  11.3 49.4 %all-gather.5.cloned.1.call-start = ((), (), s32[]{:S(2)}) async-start(), calls=%async_computation.2 | async-start | bytes 25165824 | tf_op jit(solution)/shard_map/all_gather | solution.py:13
  12.1 452.3 %reduce-scatter.2.cloned.1.call-start = ((), (), s32[]{:S(2)}) async-start(), calls=%async_computation.3 | async-start | bytes 4456448 | tf_op jit(solution)/shard_map/reduce_scatter | solution.py:35
  73.9 6.8 %copy-start = (f32[512,2048]{1,0:T(8,128)}, f32[512,2048]{1,0:T(8,128)S(1)}, u32[]{:S(2)}) copy-start(f32[512,2048]{1,0:T(8,128)S(1)} %fusion.47) | copy-start | bytes 12582916
  80.7 25.4 %collective-permute-start = (f32[512,512]{0,1:T(8,128)S(1)}, f32[512,512]{0,1:T(8,128)S(1)}, u32[]{:S(2)}, u32[]{:S(2)}) collective-permute-start(f32[512,512]{0,1:T(8,128)S(1)} %fusion.48), channel_id=1, source_target_pairs={{0,2},{2,0},{4,6},{6,4},{8,10},{10,8},{12,14},{14,12},{16,18},{18,... | collective-permute-start | bytes 3145736 | tf_op jit(solution)/shard_map/ppermute | solution.py:20
  106.3 24.6 %collective-permute-start.1 = (f32[512,512]{0,1:T(8,128)S(1)}, f32[512,512]{0,1:T(8,128)S(1)}, u32[]{:S(2)}, u32[]{:S(2)}) collective-permute-start(f32[512,512]{0,1:T(8,128)S(1)} %add.79), channel_id=1, source_target_pairs={{0,4},{2,6},{4,0},{6,2},{8,12},{10,14},{12,8},{14,10},{16,20},{18,... | collective-permute-start | bytes 3145736 | tf_op jit(solution)/shard_map/ppermute | solution.py:20
  131.1 23.7 %collective-permute-start.2 = (f32[512,512]{0,1:T(8,128)S(1)}, f32[512,512]{0,1:T(8,128)S(1)}, u32[]{:S(2)}, u32[]{:S(2)}) collective-permute-start(f32[512,512]{0,1:T(8,128)S(1)} %add.80), channel_id=1, source_target_pairs={{0,8},{2,10},{4,12},{6,14},{8,0},{10,2},{12,4},{14,6},{16,24},{18,... | collective-permute-start | bytes 3145736 | tf_op jit(solution)/shard_map/ppermute | solution.py:20
  155.1 46.3 %collective-permute-start.3 = (f32[512,512]{0,1:T(8,128)S(1)}, f32[512,512]{0,1:T(8,128)}, u32[]{:S(2)}, u32[]{:S(2)}) collective-permute-start(f32[512,512]{0,1:T(8,128)S(1)} %add.81), channel_id=1, source_target_pairs={{0,16},{2,18},{4,20},{6,22},{8,24},{10,26},{12,28},{14,30},{16,0},... | collective-permute-start | bytes 3145736 | tf_op jit(solution)/shard_map/ppermute | solution.py:20
  203.3 1.0 copy-start.3
  342.0 3.1 copy-start.1
  344.0 17.6 %slice-start = ((s8[8388608]{0:T(1024)(128)(4,1)}), s8[4194304]{0:T(1024)(128)(4,1)S(1)}, s32[]{:S(2)}) async-start(s8[8388608]{0:T(1024)(128)(4,1)} %bitcast.57), calls=%async_computation.4 | async-start | bytes 8388608
  345.1 16.5 %slice-start.1 = ((s8[8388608]{0:T(1024)(128)(4,1)}), s8[4194304]{0:T(1024)(128)(4,1)S(1)}, s32[]{:S(2)}) async-start(s8[8388608]{0:T(1024)(128)(4,1)} %bitcast.57), calls=%async_computation.5 | async-start | bytes 8388608
  359.7 1.9 copy-start.2
Sparse Core Ops, SparseCore 0:
  11.4 16.3 all-gather.2
  29.4 31.2 all-gather.4
  368.0 96.2 reduce-scatter.1
